TPU v7x, 32 devices: a whole 2x2x4 slice. The times are simulated.
32 devices in a mesh: groups: 2 (over y), ctx: 4 (over z), mp: 4 (over x, core).
Axes of the slice: x: 2, y: 2, z: 4, core: 2. Of those that a mesh axis runs over, the one named last changes fastest.
Arguments:
- queries: bfloat16 [2048, 4096], P(('groups', 'ctx'), 'mp'), parts along dimension 0, may hold values from -18 to 18
- keyvals: bfloat16 [2048, 512], P(('groups', 'ctx', 'mp')), parts along dimension 0, may hold values from -6 to 6
- segment_ids: int32 [2048], P('groups'), parts along dimension 0, may hold values from 0 to 2, never falling along the last dimension, each value on 1 to 512 neighbouring positions
- residual: bfloat16 [2048, 4096], P(('groups', 'ctx', 'mp')), parts along dimension 0, may hold values from -180 to 180
- out_weight: bfloat16 [4096, 4096], P('mp', 'ctx'), may hold values from -0.375 to 0.375
- lru_weight: bfloat16 [4096, 4096], P('ctx', 'mp'), may hold values from -0.09375 to 0.09375
- conv_weight: float32 [4, 4096], P(None, 'mp'), may hold values from -3 to 3
- gate_decay_w: bfloat16 [16, 256, 256], P('mp'), may hold values from -0.375 to 0.375
- gate_input_w: bfloat16 [16, 256, 256], P('mp'), may hold values from -0.375 to 0.375
- gate_decay_b: float32 [4096], P('mp'), may hold values from -3 to 3
- gate_input_b: float32 [4096], P('mp'), may hold values from -3 to 3
- decay_codes: int32 [4096], P('mp'), may hold values from 0 to 15
- norm_gain: float32 [4096], replicated, may hold values from 0.1 to 1.9
Outputs:
- resid_out: bfloat16 [2048, 4096], P(('groups', 'ctx', 'mp')), parts along dimension 0
- lru_out: bfloat16 [2048, 4096], P(('groups', 'ctx'), 'mp'), parts along dimension 0
There are 2 independent parts, one for each index of `groups`. A program takes and returns all parts, laid end to end along the dimension named above; an argument that names none is the same for every part. Nothing has to cross between parts.
All inputs are finite; a program needn't handle non-finite values.
Results may differ from a plain program's by a relative error of at most 0.017.
Values may be sent and summed in bfloat16 or wider, within the bound.
No kernel may reach another device: no remote copies, remote signals or barrier semaphores. Data moves between devices by JAX's collectives and lax.ppermute only.
A program may use at most 64 MiB of HBM per device.

v0:
```python
import math
import jax
import jax.numpy as jnp
from jax import lax
from jax.sharding import PartitionSpec as P

HD = 256
WIN = 2048
CONV = 4
LEVELS = 16
BW = 256


def shifted_2(value, axis, steps):
    count = lax.axis_size(axis)
    initial, last = (max(0, -steps), min(count, count - steps))
    return lax.ppermute(value, axis, [(source, source + steps) for source in range(initial, last)])


def decay_rates():
    levels = jnp.arange(LEVELS, dtype=jnp.float32)
    return 0.006 * jnp.exp(-levels * (math.log(3000.0) / (LEVELS - 1)))


def chain_link(former, latter):
    return (former[0] * latter[0], latter[0] * former[1] + latter[1])


def rms_scaled(values, norm_gain):
    value_f32 = values.astype(jnp.float32)
    inverse = lax.rsqrt(jnp.mean(value_f32 * value_f32, axis=-1, keepdims=True) + 1e-06)
    return (value_f32 * inverse * norm_gain).astype(jnp.bfloat16)


def attend_local(queries, keys_all, allowed):
    rows_here = queries.shape[0]
    heads_here = queries.shape[1] // HD
    query_heads = queries.reshape(rows_here, heads_here, HD)
    score_scale = 1.0 / math.sqrt(HD)
    scores = (
        jnp.einsum("thd,kd->htk", query_heads, keys_all[:, :HD], preferred_element_type=jnp.float32)
        * score_scale
    )
    scores = jnp.where(allowed[None], scores, -1e30)
    row_top = jnp.max(scores, axis=-1, keepdims=True)
    weights = jnp.exp(scores - row_top)
    probs = (weights / jnp.sum(weights, axis=-1, keepdims=True)).astype(jnp.bfloat16)
    gathered = jnp.einsum(
        "htk,kd->thd", probs, keys_all[:, HD:], preferred_element_type=jnp.float32
    )
    return gathered.reshape(rows_here, heads_here * HD).astype(jnp.bfloat16)


def local(
    queries,
    keyvals,
    segment_ids,
    residual,
    out_weight,
    lru_weight,
    conv_weight,
    gate_decay_w,
    gate_input_w,
    gate_decay_b,
    gate_input_b,
    decay_codes,
    norm_gain,
):
    rows_here = queries.shape[0]
    ctx_index = lax.axis_index("ctx")
    back_blocks = WIN // rows_here
    own_kv = lax.all_gather(keyvals, "mp", axis=0, tiled=True)
    earlier = []
    moving = own_kv
    for offset in range(back_blocks):
        moving = shifted_2(moving, "ctx", 1)
        earlier = [moving] + earlier
    keys_all = jnp.concatenate(earlier + [own_kv], axis=0)
    pad_seg = jnp.concatenate([jnp.full((WIN,), -1, jnp.int32), segment_ids])
    query_seg = lax.dynamic_slice_in_dim(segment_ids, ctx_index * rows_here, rows_here)
    key_seg = lax.dynamic_slice_in_dim(
        pad_seg, ctx_index * rows_here, (back_blocks + 1) * rows_here
    )
    query_pos = ctx_index * rows_here + jnp.arange(rows_here, dtype=jnp.int32)
    key_pos = (ctx_index - back_blocks) * rows_here + jnp.arange(
        (back_blocks + 1) * rows_here, dtype=jnp.int32
    )
    distance = query_pos[:, None] - key_pos[None, :]
    allowed = (distance >= 0) & (distance < WIN) & (query_seg[:, None] == key_seg[None, :])
    attended = attend_local(queries, keys_all, allowed)
    head_part = jnp.dot(
        attended,
        lax.all_gather(out_weight, "ctx", axis=1, tiled=True),
        preferred_element_type=jnp.float32,
    )
    summed = lax.psum_scatter(
        head_part.astype(jnp.bfloat16), "mp", scatter_dimension=0, tiled=True
    ).astype(jnp.float32)
    resid_out = (summed + residual.astype(jnp.float32)).astype(jnp.bfloat16)
    normed = lax.all_gather(rms_scaled(resid_out, norm_gain), "mp", axis=0, tiled=True)
    channels = lru_weight.shape[1]
    lru_in = jnp.dot(
        normed,
        lax.all_gather(lru_weight, "ctx", axis=0, tiled=True),
        preferred_element_type=jnp.float32,
    ).astype(jnp.bfloat16)
    rim_rows = shifted_2(lru_in[rows_here - (CONV - 1) :], "ctx", 1)
    extended = jnp.concatenate([rim_rows, lru_in], axis=0)
    ext_seg = lax.dynamic_slice_in_dim(
        pad_seg, ctx_index * rows_here + WIN - (CONV - 1), rows_here + CONV - 1
    )
    conv_acc = jnp.zeros((rows_here, channels), jnp.float32)
    for offset in range(CONV):
        lag_rows = CONV - 1 - offset
        shifted = extended[lag_rows : lag_rows + rows_here].astype(jnp.float32)
        same_doc = (ext_seg[lag_rows : lag_rows + rows_here] == query_seg)[:, None]
        conv_acc = conv_acc + jnp.where(same_doc, conv_weight[offset] * shifted, 0.0)
    conv_out = conv_acc.astype(jnp.bfloat16)
    blocks_here = channels // BW
    grouped = conv_out.reshape(rows_here, blocks_here, BW)
    decay_gate = jax.nn.sigmoid(
        jnp.einsum(
            "tbi,bij->tbj", grouped, gate_decay_w, preferred_element_type=jnp.float32
        ).reshape(rows_here, channels)
        + gate_decay_b
    )
    input_gate = jax.nn.sigmoid(
        jnp.einsum(
            "tbi,bij->tbj", grouped, gate_input_w, preferred_element_type=jnp.float32
        ).reshape(rows_here, channels)
        + gate_input_b
    )
    levels = jnp.arange(LEVELS, dtype=jnp.int32)
    decay_rate = jnp.sum(
        jnp.where(decay_codes[:, None] == levels[None, :], decay_rates()[None, :], 0.0), axis=1
    )
    log_decay = -8.0 * decay_gate * decay_rate
    restart = (query_seg != ext_seg[CONV - 2 : CONV - 2 + rows_here])[:, None]
    keep_factor = jnp.where(restart, 0.0, jnp.exp(log_decay))
    input_scale = jnp.where(restart, 1.0, jnp.sqrt(-jnp.expm1(2.0 * log_decay)))
    driven = input_scale * input_gate * conv_out.astype(jnp.float32)
    cum_keep, local_state = lax.associative_scan(chain_link, (keep_factor, driven), axis=0)
    block_keep = cum_keep[rows_here - 1]
    block_state = local_state[rows_here - 1]

    def relay_turn(turn_index, state_in):
        return shifted_2(block_keep * state_in + block_state, "ctx", 1)

    incoming = lax.fori_loop(0, lax.axis_size("ctx") - 1, relay_turn, jnp.zeros_like(block_state))
    states = local_state + cum_keep * incoming[None, :]
    return (resid_out, states.astype(jnp.bfloat16))


def solution(mesh):
    in_specs = (
        P(("groups", "ctx"), "mp"),
        P(("groups", "ctx", "mp"), None),
        P("groups"),
        P(("groups", "ctx", "mp"), None),
        P("mp", "ctx"),
        P("ctx", "mp"),
        P(None, "mp"),
        P("mp", None, None),
        P("mp", None, None),
        P("mp"),
        P("mp"),
        P("mp"),
        P(),
    )
    out_specs = (P(("groups", "ctx", "mp"), None), P(("groups", "ctx"), "mp"))
    return jax.shard_map(local, mesh=mesh, in_specs=in_specs, out_specs=out_specs, check_vma=False)
```

profile of v0, /device:TPU:0, one launch (start us, length us, event | category | flops | bytes accessed | tf_op | source)
XLA Modules:
  0.0 554.3 jit_solution(5232723126797398906)
XLA Ops:
  8.0 7.4 %all_gather.12 = bf16[256,512]{1,0:T(8,128)(2,1)S(1)} all-gather(bf16[64,512]{1,0:T(8,128)(2,1)} %param.16), channel_id=1, replica_groups=mesh['groups'=2,'ctx'=4,'mp'=4] {'mp'}, dimensions={0}, use_global_device_ids=true | all-gather | bytes 327680 | tf_op jit(solution)/shard_map/all_gather | solution.py:72
  15.4 3.5 collective-permute-start.1
  18.9 9.3 %collective-permute-done.1 = bf16[256,512]{1,0:T(8,128)(2,1)S(1)} collective-permute-done((bf16[256,512]{1,0:T(8,128)(2,1)S(1)}, bf16[256,512]{1,0:T(8,128)(2,1)S(1)}, u32[]{:S(2)}, u32[]{:S(2)}) %collective-permute-start.1) | collective-permute-done | bytes 262176 | tf_op jit(solution)/shard_map/ppermute | solution.py:17
  28.3 8.5 %collective-permute-start.2 = (bf16[256,512]{1,0:T(8,128)(2,1)S(1)}, bf16[256,512]{1,0:T(8,128)(2,1)S(1)}, u32[]{:S(2)}, u32[]{:S(2)}) collective-permute-start(bf16[256,512]{1,0:T(8,128)(2,1)S(1)} %collective-permute-done.1), channel_id=1, source_target_pairs={{0,4},{4,8},{8,12},{1,5},{5,9},{9,13},{2,6},{6,10},{10,14},{3,7},{... | collective-permute-start | bytes 786440 | tf_op jit(solution)/shard_map/ppermute | solution.py:17
  36.8 11.2 %collective-permute-done.2 = bf16[256,512]{1,0:T(8,128)(2,1)S(1)} collective-permute-done((bf16[256,512]{1,0:T(8,128)(2,1)S(1)}, bf16[256,512]{1,0:T(8,128)(2,1)S(1)}, u32[]{:S(2)}, u32[]{:S(2)}) %collective-permute-start.2) | collective-permute-done | bytes 262176 | tf_op jit(solution)/shard_map/ppermute | solution.py:17
  48.0 13.6 %collective-permute-start.3 = (bf16[256,512]{1,0:T(8,128)(2,1)S(1)}, bf16[256,512]{1,0:T(8,128)(2,1)S(1)}, u32[]{:S(2)}, u32[]{:S(2)}) collective-permute-start(bf16[256,512]{1,0:T(8,128)(2,1)S(1)} %collective-permute-done.2), channel_id=1, source_target_pairs={{0,4},{4,8},{8,12},{1,5},{5,9},{9,13},{2,6},{6,10},{10,14},{3,7},{... | collective-permute-start | bytes 786440 | tf_op jit(solution)/shard_map/ppermute | solution.py:17
  61.6 10.2 %collective-permute-done.3 = bf16[256,512]{1,0:T(8,128)(2,1)S(1)} collective-permute-done((bf16[256,512]{1,0:T(8,128)(2,1)S(1)}, bf16[256,512]{1,0:T(8,128)(2,1)S(1)}, u32[]{:S(2)}, u32[]{:S(2)}) %collective-permute-start.3) | collective-permute-done | bytes 262176 | tf_op jit(solution)/shard_map/ppermute | solution.py:17
  71.8 12.3 %collective-permute-start.4 = (bf16[256,512]{1,0:T(8,128)(2,1)S(1)}, bf16[256,512]{1,0:T(8,128)(2,1)S(1)}, u32[]{:S(2)}, u32[]{:S(2)}) collective-permute-start(bf16[256,512]{1,0:T(8,128)(2,1)S(1)} %collective-permute-done.3), channel_id=1, source_target_pairs={{0,4},{4,8},{8,12},{1,5},{5,9},{9,13},{2,6},{6,10},{10,14},{3,7},{... | collective-permute-start | bytes 786440 | tf_op jit(solution)/shard_map/ppermute | solution.py:17
  84.1 9.6 %collective-permute-done.4 = bf16[256,512]{1,0:T(8,128)(2,1)S(1)} collective-permute-done((bf16[256,512]{1,0:T(8,128)(2,1)S(1)}, bf16[256,512]{1,0:T(8,128)(2,1)S(1)}, u32[]{:S(2)}, u32[]{:S(2)}) %collective-permute-start.4) | collective-permute-done | bytes 262176 | tf_op jit(solution)/shard_map/ppermute | solution.py:17
  93.7 11.3 %collective-permute-start.5 = (bf16[256,512]{1,0:T(8,128)(2,1)S(1)}, bf16[256,512]{1,0:T(8,128)(2,1)S(1)}, u32[]{:S(2)}, u32[]{:S(2)}) collective-permute-start(bf16[256,512]{1,0:T(8,128)(2,1)S(1)} %collective-permute-done.4), channel_id=1, source_target_pairs={{0,4},{4,8},{8,12},{1,5},{5,9},{9,13},{2,6},{6,10},{10,14},{3,7},{... | collective-permute-start | bytes 786440 | tf_op jit(solution)/shard_map/ppermute | solution.py:17
  105.0 9.7 %collective-permute-done.5 = bf16[256,512]{1,0:T(8,128)(2,1)S(1)} collective-permute-done((bf16[256,512]{1,0:T(8,128)(2,1)S(1)}, bf16[256,512]{1,0:T(8,128)(2,1)S(1)}, u32[]{:S(2)}, u32[]{:S(2)}) %collective-permute-start.5) | collective-permute-done | bytes 262176 | tf_op jit(solution)/shard_map/ppermute | solution.py:17
  114.6 13.8 %collective-permute-start.6 = (bf16[256,512]{1,0:T(8,128)(2,1)S(1)}, bf16[256,512]{1,0:T(8,128)(2,1)S(1)}, u32[]{:S(2)}, u32[]{:S(2)}) collective-permute-start(bf16[256,512]{1,0:T(8,128)(2,1)S(1)} %collective-permute-done.5), channel_id=1, source_target_pairs={{0,4},{4,8},{8,12},{1,5},{5,9},{9,13},{2,6},{6,10},{10,14},{3,7},{... | collective-permute-start | bytes 786440 | tf_op jit(solution)/shard_map/ppermute | solution.py:17
  128.7 9.4 %collective-permute-done.6 = bf16[256,512]{1,0:T(8,128)(2,1)S(1)} collective-permute-done((bf16[256,512]{1,0:T(8,128)(2,1)S(1)}, bf16[256,512]{1,0:T(8,128)(2,1)S(1)}, u32[]{:S(2)}, u32[]{:S(2)}) %collective-permute-start.6) | collective-permute-done | bytes 262176 | tf_op jit(solution)/shard_map/ppermute | solution.py:17
  138.1 9.9 %collective-permute-start.7 = (bf16[256,512]{1,0:T(8,128)(2,1)S(1)}, bf16[256,512]{1,0:T(8,128)(2,1)S(1)}, u32[]{:S(2)}, u32[]{:S(2)}) collective-permute-start(bf16[256,512]{1,0:T(8,128)(2,1)S(1)} %collective-permute-done.6), channel_id=1, source_target_pairs={{0,4},{4,8},{8,12},{1,5},{5,9},{9,13},{2,6},{6,10},{10,14},{3,7},{... | collective-permute-start | bytes 786440 | tf_op jit(solution)/shard_map/ppermute | solution.py:17
  148.1 9.5 %collective-permute-done.7 = bf16[256,512]{1,0:T(8,128)(2,1)S(1)} collective-permute-done((bf16[256,512]{1,0:T(8,128)(2,1)S(1)}, bf16[256,512]{1,0:T(8,128)(2,1)S(1)}, u32[]{:S(2)}, u32[]{:S(2)}) %collective-permute-start.7) | collective-permute-done | bytes 262176 | tf_op jit(solution)/shard_map/ppermute | solution.py:17
  157.6 13.0 %collective-permute-start.8 = (bf16[256,512]{1,0:T(8,128)(2,1)S(1)}, bf16[256,512]{1,0:T(8,128)(2,1)S(1)}, u32[]{:S(2)}, u32[]{:S(2)}) collective-permute-start(bf16[256,512]{1,0:T(8,128)(2,1)S(1)} %collective-permute-done.7), channel_id=1, source_target_pairs={{0,4},{4,8},{8,12},{1,5},{5,9},{9,13},{2,6},{6,10},{10,14},{3,7},{... | collective-permute-start | bytes 786440 | tf_op jit(solution)/shard_map/ppermute | solution.py:17
  170.6 1.6 fusion.7
  172.2 8.0 %collective-permute-done.8 = bf16[256,512]{1,0:T(8,128)(2,1)S(1)} collective-permute-done((bf16[256,512]{1,0:T(8,128)(2,1)S(1)}, bf16[256,512]{1,0:T(8,128)(2,1)S(1)}, u32[]{:S(2)}, u32[]{:S(2)}) %collective-permute-start.8) | collective-permute-done | bytes 262176 | tf_op jit(solution)/shard_map/ppermute | solution.py:17
  181.8 4.7 fusion.53
  186.5 6.0 %fusion.8 = bf16[256,4,256]{2,0,1:T(8,128)(2,1)S(1)} fusion(f32[4,256]{1,0:T(4,128)S(1)} %fusion.53, bf16[2304,512]{1,0:T(8,128)(2,1)} %copy-done.12, pred[256,2304]{0,1:T(8,128)(4,1)S(1)} %fusion.7, bf16[32,4,8,256]{3,2,1,0:T(8,128)(2,1)S(1)} %bitcast.79), kind=kOutput, calls=%fused_computation.17 | convolution fusion | flops 2427981056 | bytes 4001792 | tf_op jit(solution)/shard_map/htk,kd->thd/dot_general | solution.py:48
  192.5 6.9 %all-gather.4.cloned.1.call-done = bf16[1024,4096]{1,0:T(8,128)(2,1)} async-done(((bf16[1024,1024]{1,0:T(8,128)(2,1)}), bf16[1024,4096]{1,0:T(8,128)(2,1)}) %all-gather.4.cloned.1.call-update) | async-done | bytes 8388624 | tf_op jit(solution)/shard_map/all_gather | solution.py:93
  199.5 7.1 %convolution_convert_fusion = bf16[256,4096]{1,0:T(8,128)(2,1)} fusion(bf16[256,1024]{0,1:T(8,128)(2,1)S(1)} %bitcast.71, bf16[1024,4096]{1,0:T(8,128)(2,1)} %all-gather.4.cloned.1.call-done), kind=kOutput, calls=%fused_computation.6 | convolution fusion | flops 2148532224 | bytes 11010048 | tf_op jit(solution)/shard_map/dot_general | solution.py:91
  207.6 33.9 %reduce-scatter.2.cloned.1.call-done = bf16[64,4096]{1,0:T(8,128)(2,1)} async-done(((bf16[256,4096]{1,0:T(8,128)(2,1)}), bf16[64,4096]{1,0:T(8,128)(2,1)}) %reduce-scatter.2.cloned.1.call-update) | async-done | bytes 524304 | tf_op jit(solution)/shard_map/reduce_scatter | solution.py:96
  244.8 147.9 %all-gather.8.cloned.1.call-done = bf16[4096,1024]{1,0:T(8,128)(2,1)} async-done(((bf16[1024,1024]{1,0:T(8,128)(2,1)}), bf16[4096,1024]{1,0:T(8,128)(2,1)}) %all-gather.8.cloned.1.call-update) | async-done | bytes 8388624 | tf_op jit(solution)/shard_map/all_gather | solution.py:104
  392.8 22.8 %all-gather.6.cloned.1.call-done = bf16[256,4096]{1,0:T(8,128)(2,1)} async-done(((bf16[64,4096]{1,0:T(8,128)(2,1)}), bf16[256,4096]{1,0:T(8,128)(2,1)}) %all-gather.6.cloned.1.call-update) | async-done | bytes 2097168 | tf_op jit(solution)/shard_map/all_gather | solution.py:100
  415.5 6.3 %convolution_convert_fusion.1 = bf16[256,1024]{1,0:T(8,128)(2,1)S(1)} fusion(bf16[256,4096]{1,0:T(8,128)(2,1)} %all-gather.6.cloned.1.call-done, bf16[4096,1024]{1,0:T(8,128)(2,1)} %all-gather.8.cloned.1.call-done), kind=kOutput, calls=%fused_computation.18 | convolution fusion | flops 2147745792 | bytes 11010048 | tf_op jit(solution)/shard_map/dot_general | solution.py:102
  421.9 3.4 collective-permute-start.9
  430.8 2.8 convert_multiply_fusion.2
  439.4 2.5 multiply_add_fusion.1
  441.9 1.7 slice.302
  443.6 1.7 slice.303
  446.8 1.9 multiply_add_fusion.2
  450.1 1.6 slice.307
  451.7 1.6 slice.311
  453.4 1.8 multiply_add_fusion.3
  459.5 1.6 multiply_add_fusion.4
  492.8 1.5 slice.312
  500.8 1.7 slice.349
  504.5 1.5 slice.294
  515.7 2.7 pad.114
  518.6 2.3 fusion.24
  521.1 2.7 pad.130
  525.0 2.7 pad.129
  528.5 16.5 %while.10 = (s32[]{:T(128)}, f32[1024]{0:T(1024)S(1)}, f32[1024]{0:T(1024)S(1)}, f32[1024]{0:T(1024)S(1)}, s32[]{:T(128)}) while((s32[]{:T(128)}, f32[1024]{0:T(1024)S(1)}, f32[1024]{0:T(1024)S(1)}, f32[1024]{0:T(1024)S(1)}, s32[]{:T(128)}) %tuple.63), condition=%wide.region_6.7_spmd, body=%wide.region_5.6_spmd.sunk | while | flops 2050 | bytes 32869 | solution.py:149
  528.5 4.2 collective-permute-start
  534.0 4.2 collective-permute-start
  539.5 4.2 collective-permute-start
  545.0 2.8 add_convert_fusion
  (211 shorter events, 80.8 us)
Async XLA Ops:
  7.2 420.2 %copy-start = (bf16[4,256,256]{2,1,0:T(8,128)(2,1)S(1)}, bf16[4,256,256]{2,1,0:T(8,128)(2,1)}, u32[]{:S(2)}) copy-start(bf16[4,256,256]{2,1,0:T(8,128)(2,1)} %param.22) | copy-start | bytes 1572868
  7.2 121.3 %copy-start.13 = (s32[1024]{0:T(1024)S(1)}, s32[1024]{0:T(1024)}, u32[]{:S(2)}) copy-start(s32[1024]{0:T(1024)} %param.17) | copy-start | bytes 12292
  7.2 192.3 %all-gather.4.cloned.1.call-start = ((), (), s32[]{:S(2)}) async-start(), calls=%async_computation.1 | async-start | bytes 10485760 | tf_op jit(solution)/shard_map/all_gather | solution.py:93
  7.9 233.6 %reduce-scatter.2.cloned.1.call-start = ((), (), s32[]{:S(2)}) async-start(), calls=%async_computation.2 | async-start | bytes 2621440 | tf_op jit(solution)/shard_map/reduce_scatter | solution.py:96
  15.4 12.9 %collective-permute-start.1 = (bf16[256,512]{1,0:T(8,128)(2,1)S(1)}, bf16[256,512]{1,0:T(8,128)(2,1)S(1)}, u32[]{:S(2)}, u32[]{:S(2)}) collective-permute-start(bf16[256,512]{1,0:T(8,128)(2,1)S(1)} %all_gather.12), channel_id=1, source_target_pairs={{0,4},{4,8},{8,12},{1,5},{5,9},{9,13},{2,6},{6,10},{10,14},{3,7},{... | collective-permute-start | bytes 786440 | tf_op jit(solution)/shard_map/ppermute | solution.py:17
  28.3 19.7 %collective-permute-start.2 = (bf16[256,512]{1,0:T(8,128)(2,1)S(1)}, bf16[256,512]{1,0:T(8,128)(2,1)S(1)}, u32[]{:S(2)}, u32[]{:S(2)}) collective-permute-start(bf16[256,512]{1,0:T(8,128)(2,1)S(1)} %collective-permute-done.1), channel_id=1, source_target_pairs={{0,4},{4,8},{8,12},{1,5},{5,9},{9,13},{2,6},{6,10},{10,14},{3,7},{... | collective-permute-start | bytes 786440 | tf_op jit(solution)/shard_map/ppermute | solution.py:17
  48.0 23.8 %collective-permute-start.3 = (bf16[256,512]{1,0:T(8,128)(2,1)S(1)}, bf16[256,512]{1,0:T(8,128)(2,1)S(1)}, u32[]{:S(2)}, u32[]{:S(2)}) collective-permute-start(bf16[256,512]{1,0:T(8,128)(2,1)S(1)} %collective-permute-done.2), channel_id=1, source_target_pairs={{0,4},{4,8},{8,12},{1,5},{5,9},{9,13},{2,6},{6,10},{10,14},{3,7},{... | collective-permute-start | bytes 786440 | tf_op jit(solution)/shard_map/ppermute | solution.py:17
  71.8 21.9 %collective-permute-start.4 = (bf16[256,512]{1,0:T(8,128)(2,1)S(1)}, bf16[256,512]{1,0:T(8,128)(2,1)S(1)}, u32[]{:S(2)}, u32[]{:S(2)}) collective-permute-start(bf16[256,512]{1,0:T(8,128)(2,1)S(1)} %collective-permute-done.3), channel_id=1, source_target_pairs={{0,4},{4,8},{8,12},{1,5},{5,9},{9,13},{2,6},{6,10},{10,14},{3,7},{... | collective-permute-start | bytes 786440 | tf_op jit(solution)/shard_map/ppermute | solution.py:17
  93.7 21.0 %collective-permute-start.5 = (bf16[256,512]{1,0:T(8,128)(2,1)S(1)}, bf16[256,512]{1,0:T(8,128)(2,1)S(1)}, u32[]{:S(2)}, u32[]{:S(2)}) collective-permute-start(bf16[256,512]{1,0:T(8,128)(2,1)S(1)} %collective-permute-done.4), channel_id=1, source_target_pairs={{0,4},{4,8},{8,12},{1,5},{5,9},{9,13},{2,6},{6,10},{10,14},{3,7},{... | collective-permute-start | bytes 786440 | tf_op jit(solution)/shard_map/ppermute | solution.py:17
  114.6 23.4 %collective-permute-start.6 = (bf16[256,512]{1,0:T(8,128)(2,1)S(1)}, bf16[256,512]{1,0:T(8,128)(2,1)S(1)}, u32[]{:S(2)}, u32[]{:S(2)}) collective-permute-start(bf16[256,512]{1,0:T(8,128)(2,1)S(1)} %collective-permute-done.5), channel_id=1, source_target_pairs={{0,4},{4,8},{8,12},{1,5},{5,9},{9,13},{2,6},{6,10},{10,14},{3,7},{... | collective-permute-start | bytes 786440 | tf_op jit(solution)/shard_map/ppermute | solution.py:17
  138.1 19.5 %collective-permute-start.7 = (bf16[256,512]{1,0:T(8,128)(2,1)S(1)}, bf16[256,512]{1,0:T(8,128)(2,1)S(1)}, u32[]{:S(2)}, u32[]{:S(2)}) collective-permute-start(bf16[256,512]{1,0:T(8,128)(2,1)S(1)} %collective-permute-done.6), channel_id=1, source_target_pairs={{0,4},{4,8},{8,12},{1,5},{5,9},{9,13},{2,6},{6,10},{10,14},{3,7},{... | collective-permute-start | bytes 786440 | tf_op jit(solution)/shard_map/ppermute | solution.py:17
  157.6 22.6 %collective-permute-start.8 = (bf16[256,512]{1,0:T(8,128)(2,1)S(1)}, bf16[256,512]{1,0:T(8,128)(2,1)S(1)}, u32[]{:S(2)}, u32[]{:S(2)}) collective-permute-start(bf16[256,512]{1,0:T(8,128)(2,1)S(1)} %collective-permute-done.7), channel_id=1, source_target_pairs={{0,4},{4,8},{8,12},{1,5},{5,9},{9,13},{2,6},{6,10},{10,14},{3,7},{... | collective-permute-start | bytes 786440 | tf_op jit(solution)/shard_map/ppermute | solution.py:17
  180.4 1.4 copy-start.12
  181.8 4.7 copy-start.28
  206.5 35.0 %copy-start.4 = (bf16[64,4096]{1,0:T(8,128)(2,1)S(1)}, bf16[64,4096]{1,0:T(8,128)(2,1)}, u32[]{:S(2)}) copy-start(bf16[64,4096]{1,0:T(8,128)(2,1)} %param.18) | copy-start | bytes 1572868
  206.6 37.1 %copy-start.14 = (f32[4096]{0:T(1024)S(1)}, f32[4096]{0:T(1024)}, u32[]{:S(2)}) copy-start(f32[4096]{0:T(1024)} %param.27) | copy-start | bytes 49156
  206.6 38.1 %copy-start.25 = (s32[1024]{0:T(1024)S(1)}, s32[1024]{0:T(1024)}, u32[]{:S(2)}) copy-start(s32[1024]{0:T(1024)} %param.26) | copy-start | bytes 12292
  206.6 38.2 %copy-start.24 = (f32[4,1024]{1,0:T(4,128)S(1)}, f32[4,1024]{1,0:T(4,128)}, u32[]{:S(2)}) copy-start(f32[4,1024]{1,0:T(4,128)} %param.21) | copy-start | bytes 49156
  206.6 186.1 %all-gather.8.cloned.1.call-start = ((), (), s32[]{:S(2)}) async-start(), calls=%async_computation.4 | async-start | bytes 10485760 | tf_op jit(solution)/shard_map/all_gather | solution.py:104
  207.3 208.2 %all-gather.6.cloned.1.call-start = ((), (), s32[]{:S(2)}) async-start(), calls=%async_computation.3 | async-start | bytes 2621440 | tf_op jit(solution)/shard_map/all_gather | solution.py:100
  242.9 0.8 copy-start.2
  421.9 4.7 collective-permute-start.9
  427.4 1.7 copy-start.5
  429.1 1.7 copy-start.26
  429.1 1.7 copy-start.27
  504.4 7.2 %copy-start.11 = (f32[3,1024]{1,0:T(4,128)S(1)}, f32[3,1024]{1,0:T(4,128)}, u32[]{:S(2)}) copy-start(f32[3,1024]{1,0:T(4,128)} %slice.341) | copy-start | bytes 36868
  504.4 7.2 %copy-start.23 = (f32[1,1024]{1,0:T(1,128)S(1)}, f32[1,1024]{1,0:T(1,128)}, u32[]{:S(2)}) copy-start(f32[1,1024]{1,0:T(1,128)} %slice.407) | copy-start | bytes 12292
  504.4 7.3 %copy-start.22 = (f32[1,1024]{1,0:T(1,128)S(1)}, f32[1,1024]{1,0:T(1,128)}, u32[]{:S(2)}) copy-start(f32[1,1024]{1,0:T(1,128)} %slice.381) | copy-start | bytes 12292
  504.4 7.4 %copy-start.9 = (f32[7,1024]{1,0:T(8,128)S(1)}, f32[7,1024]{1,0:T(8,128)}, u32[]{:S(2)}) copy-start(f32[7,1024]{1,0:T(8,128)} %slice.318) | copy-start | bytes 86020
  504.4 7.4 %copy-start.10 = (f32[7,1024]{1,0:T(8,128)S(1)}, f32[7,1024]{1,0:T(8,128)}, u32[]{:S(2)}) copy-start(f32[7,1024]{1,0:T(8,128)} %slice.343) | copy-start | bytes 86020
  504.4 8.9 %copy-start.7 = (f32[15,1024]{1,0:T(8,128)S(1)}, f32[15,1024]{1,0:T(8,128)}, u32[]{:S(2)}) copy-start(f32[15,1024]{1,0:T(8,128)} %slice.312) | copy-start | bytes 184324
  504.4 8.9 %copy-start.8 = (f32[15,1024]{1,0:T(8,128)S(1)}, f32[15,1024]{1,0:T(8,128)}, u32[]{:S(2)}) copy-start(f32[15,1024]{1,0:T(8,128)} %slice.345) | copy-start | bytes 184324
  507.5 6.8 %copy-start.6 = (f32[31,1024]{1,0:T(8,128)S(1)}, f32[31,1024]{1,0:T(8,128)}, u32[]{:S(2)}) copy-start(f32[31,1024]{1,0:T(8,128)} %slice.347) | copy-start | bytes 380932
  508.1 5.3 copy-start.21
  511.8 2.6 copy-start.20
  513.4 1.2 copy-start.19
  514.3 1.0 copy-start.3
  514.5 0.9 copy-start.18
  515.4 2.9 copy-start.17
  518.6 2.3 copy-start.16
  520.9 3.0 copy-start.15
  521.1 6.6 %copy-start.1 = (f32[256,1024]{1,0:T(8,128)S(1)}, f32[256,1024]{1,0:T(8,128)}, u32[]{:S(2)}) copy-start(f32[256,1024]{1,0:T(8,128)} %pad.114) | copy-start | bytes 3145732
  528.5 5.5 collective-permute-start
  534.0 5.5 collective-permute-start
  539.5 5.5 collective-permute-start
Sparse Core Ops, SparseCore 0:
  9.6 189.8 all-gather.3
  206.7 34.7 reduce-scatter.1
  243.1 149.6 all-gather.7
  394.7 20.7 all-gather.5
where the time goes:
time: 557 us; the launch traced here: 554 us
  waiting for transfers between devices  295 us (53%)
  starting transfers between devices  102 us (18%)
  local copies, waits for them, and re-layouts  77.2 us (14%)
  other arithmetic  32.9 us (6%)
  matrix products  24.8 us (4%)
  between operations  14.7 us (3%)
  blocking collectives  7.43 us (1%)
    all_gather x1, waiting for transfers between devices, local(): lax.all_gather(lru_weight, 'ctx', axis=0, tiled=True)  148 us
    ppermute x12, starting transfers between devices, shifted_2(): lax.ppermute(value, axis, [(source, source + steps) for source in range(i...  102 us
    ppermute x12, waiting for transfers between devices, shifted_2(): lax.ppermute(value, axis, [(source, source + steps) for source in range(i...  82.1 us
    slice x52, local copies, waits for them, and re-layouts, local(): lax.associative_scan(chain_link, (keep_factor, driven), axis=0)  61 us
    reduce_scatter x1, waiting for transfers between devices, local(): lax.psum_scatter(head_part.astype(jnp.bfloat16), 'mp', scatter_dimension=...  33.9 us
    all_gather x1, waiting for transfers between devices, local(): lax.all_gather(rms_scaled(resid_out, norm_gain), 'mp', axis=0, tiled=True)  22.8 us
    add x13, other arithmetic, chain_link(): return (former[0] * latter[0], latter[0] * former[1] + latter[1])  13.8 us
  transfers between devices with their start and end apart: 16, of which 16 were waited for; matrix products, arithmetic and copies ran while one was open for 3% of the time, Pallas kernels for 0%

commit v1 on v0

--- a/solution.py
+++ b/solution.py
@@ -1,3 +1,4 @@
+import functools
 import math
 import jax
 import jax.numpy as jnp
@@ -9,6 +10,41 @@
 CONV = 4
 LEVELS = 16
 BW = 256
+
+
+def finish_sections(local_values, which_axis, along_dim):
+    item_now, local_part, w_next = (
+        lax.axis_size(which_axis),
+        lax.axis_index(which_axis),
+        local_values.shape[along_dim],
+    )
+    store = []
+    for i, t in enumerate(local_values.shape):
+        store.append(t * item_now if i == along_dim else t)
+    k_now = lax.dynamic_update_slice_in_dim(
+        jnp.zeros(store, local_values.dtype), local_values, local_part * w_next, axis=along_dim
+    )
+    tmp = plain = local_values
+    for jj in range(1, item_now // 2 + 1):
+        by_rank = []
+        for i in range(item_now):
+            by_rank.append((i, (i + 1) % item_now))
+        tmp = lax.ppermute(tmp, axis_name=which_axis, perm=by_rank)
+        k_now = lax.dynamic_update_slice_in_dim(
+            k_now, tmp, (local_part - jj) % item_now * w_next, axis=along_dim
+        )
+        if 2 * jj < item_now:
+            fields = []
+            for i in range(item_now):
+                fields.append((i, (i - 1) % item_now))
+            plain = lax.ppermute(plain, axis_name=which_axis, perm=fields)
+            k_now = lax.dynamic_update_slice_in_dim(
+                k_now, plain, (local_part + jj) % item_now * w_next, axis=along_dim
+            )
+    return k_now
+
+
+_name_table = functools.partial(finish_sections, which_axis="ctx", along_dim=0)
 
 
 def shifted_2(value, axis, steps):
@@ -99,11 +135,9 @@
     resid_out = (summed + residual.astype(jnp.float32)).astype(jnp.bfloat16)
     normed = lax.all_gather(rms_scaled(resid_out, norm_gain), "mp", axis=0, tiled=True)
     channels = lru_weight.shape[1]
-    lru_in = jnp.dot(
-        normed,
-        lax.all_gather(lru_weight, "ctx", axis=0, tiled=True),
-        preferred_element_type=jnp.float32,
-    ).astype(jnp.bfloat16)
+    lru_in = jnp.dot(normed, _name_table(lru_weight), preferred_element_type=jnp.float32).astype(
+        jnp.bfloat16
+    )
     rim_rows = shifted_2(lru_in[rows_here - (CONV - 1) :], "ctx", 1)
     extended = jnp.concatenate([rim_rows, lru_in], axis=0)
     ext_seg = lax.dynamic_slice_in_dim(

time: 557 us -> 491 us (0.88)
  waiting for transfers between devices: 295 us -> 208 us
  local copies, waits for them, and re-layouts: 77.2 us -> 92.8 us
    all_gather x1 -> x0, waiting for transfers between devices: 148 us -> none  [local(): lax.all_gather(lru_weight, 'ctx', axis=0, tiled=True)]
    ppermute x0 -> x3, waiting for transfers between devices: none -> 86.8 us  [the longest x2 51.1 us: finish_sections(): tmp = lax.ppermute(tmp, axis_name=which_axis, perm=by_rank)]
    all_gather x1, waiting for transfers between devices: 22.8 us -> 0.01 us  [local(): lax.all_gather(rms_scaled(resid_out, norm_gain), 'mp', axis=0, tiled=True)]
    dynamic_update_slice x0 -> x4, local copies, waits for them, and re-layouts: none -> 10.9 us  [the longest x2 6.27 us: finish_sections(): lax.dynamic_update_slice_in_dim(k_now, tmp, (local_part - jj) % item_now...]
    ppermute x0 -> x3, starting transfers between devices: none -> 6.32 us  [the longest x1 3.4 us: finish_sections(): plain = lax.ppermute(plain, axis_name=which_axis, perm=fields)]
  transfers between devices with their start and end apart: 16 -> 18, of which waited for: 16 -> 17; matrix products, arithmetic and copies ran while one was open for 3% -> 6% of each run, Pallas kernels for 0% -> 0%
where the time goes in v1:
time: 491 us; the launch traced here: 488 us
  waiting for transfers between devices  208 us (42%)
  starting transfers between devices  107 us (22%)
  local copies, waits for them, and re-layouts  92.8 us (19%)
  other arithmetic  32.9 us (7%)
  matrix products  25 us (5%)
  between operations  14.7 us (3%)
  blocking collectives  7.43 us (2%)
    ppermute x12, starting transfers between devices, shifted_2(): lax.ppermute(value, axis, [(source, source + steps) for source in range(i...  100 us
    ppermute x12, waiting for transfers between devices, shifted_2(): lax.ppermute(value, axis, [(source, source + steps) for source in range(i...  82.1 us
    slice x52, local copies, waits for them, and re-layouts, local(): lax.associative_scan(chain_link, (keep_factor, driven), axis=0)  61.2 us
    ppermute x2, waiting for transfers between devices, finish_sections(): tmp = lax.ppermute(tmp, axis_name=which_axis, perm=by_rank)  51.1 us
    ppermute x1, waiting for transfers between devices, finish_sections(): plain = lax.ppermute(plain, axis_name=which_axis, perm=fields)  35.7 us
    reduce_scatter x1, waiting for transfers between devices, local(): lax.psum_scatter(head_part.astype(jnp.bfloat16), 'mp', scatter_dimension=...  32 us
    add x13, other arithmetic, chain_link(): return (former[0] * latter[0], latter[0] * former[1] + latter[1])  13.9 us
    pad x28, local copies, waits for them, and re-layouts, local(): lax.associative_scan(chain_link, (keep_factor, driven), axis=0)  10.4 us
  transfers between devices with their start and end apart: 18, of which 17 were waited for; matrix products, arithmetic and copies ran while one was open for 6% of the time, Pallas kernels for 0%

profile of v1, /device:TPU:0, one launch (start us, length us, event | category | flops | bytes accessed | tf_op | source)
XLA Modules:
  0.0 488.1 jit_solution(3460600048332218284)
XLA Ops:
  8.0 7.4 %all_gather.9 = bf16[256,512]{1,0:T(8,128)(2,1)S(1)} all-gather(bf16[64,512]{1,0:T(8,128)(2,1)} %param.16), channel_id=1, replica_groups=mesh['groups'=2,'ctx'=4,'mp'=4] {'mp'}, dimensions={0}, use_global_device_ids=true | all-gather | bytes 327680 | tf_op jit(solution)/shard_map/all_gather | solution.py:108
  15.4 3.5 collective-permute-start.1
  18.9 9.3 %collective-permute-done.1 = bf16[256,512]{1,0:T(8,128)(2,1)S(1)} collective-permute-done((bf16[256,512]{1,0:T(8,128)(2,1)S(1)}, bf16[256,512]{1,0:T(8,128)(2,1)S(1)}, u32[]{:S(2)}, u32[]{:S(2)}) %collective-permute-start.1) | collective-permute-done | bytes 262176 | tf_op jit(solution)/shard_map/ppermute | solution.py:53
  28.3 8.5 %collective-permute-start.2 = (bf16[256,512]{1,0:T(8,128)(2,1)S(1)}, bf16[256,512]{1,0:T(8,128)(2,1)S(1)}, u32[]{:S(2)}, u32[]{:S(2)}) collective-permute-start(bf16[256,512]{1,0:T(8,128)(2,1)S(1)} %collective-permute-done.1), channel_id=1, source_target_pairs={{0,4},{4,8},{8,12},{1,5},{5,9},{9,13},{2,6},{6,10},{10,14},{3,7},{... | collective-permute-start | bytes 786440 | tf_op jit(solution)/shard_map/ppermute | solution.py:53
  36.8 11.2 %collective-permute-done.2 = bf16[256,512]{1,0:T(8,128)(2,1)S(1)} collective-permute-done((bf16[256,512]{1,0:T(8,128)(2,1)S(1)}, bf16[256,512]{1,0:T(8,128)(2,1)S(1)}, u32[]{:S(2)}, u32[]{:S(2)}) %collective-permute-start.2) | collective-permute-done | bytes 262176 | tf_op jit(solution)/shard_map/ppermute | solution.py:53
  48.0 13.6 %collective-permute-start.3 = (bf16[256,512]{1,0:T(8,128)(2,1)S(1)}, bf16[256,512]{1,0:T(8,128)(2,1)S(1)}, u32[]{:S(2)}, u32[]{:S(2)}) collective-permute-start(bf16[256,512]{1,0:T(8,128)(2,1)S(1)} %collective-permute-done.2), channel_id=1, source_target_pairs={{0,4},{4,8},{8,12},{1,5},{5,9},{9,13},{2,6},{6,10},{10,14},{3,7},{... | collective-permute-start | bytes 786440 | tf_op jit(solution)/shard_map/ppermute | solution.py:53
  61.6 10.2 %collective-permute-done.3 = bf16[256,512]{1,0:T(8,128)(2,1)S(1)} collective-permute-done((bf16[256,512]{1,0:T(8,128)(2,1)S(1)}, bf16[256,512]{1,0:T(8,128)(2,1)S(1)}, u32[]{:S(2)}, u32[]{:S(2)}) %collective-permute-start.3) | collective-permute-done | bytes 262176 | tf_op jit(solution)/shard_map/ppermute | solution.py:53
  71.8 12.3 %collective-permute-start.4 = (bf16[256,512]{1,0:T(8,128)(2,1)S(1)}, bf16[256,512]{1,0:T(8,128)(2,1)S(1)}, u32[]{:S(2)}, u32[]{:S(2)}) collective-permute-start(bf16[256,512]{1,0:T(8,128)(2,1)S(1)} %collective-permute-done.3), channel_id=1, source_target_pairs={{0,4},{4,8},{8,12},{1,5},{5,9},{9,13},{2,6},{6,10},{10,14},{3,7},{... | collective-permute-start | bytes 786440 | tf_op jit(solution)/shard_map/ppermute | solution.py:53
  84.1 9.6 %collective-permute-done.4 = bf16[256,512]{1,0:T(8,128)(2,1)S(1)} collective-permute-done((bf16[256,512]{1,0:T(8,128)(2,1)S(1)}, bf16[256,512]{1,0:T(8,128)(2,1)S(1)}, u32[]{:S(2)}, u32[]{:S(2)}) %collective-permute-start.4) | collective-permute-done | bytes 262176 | tf_op jit(solution)/shard_map/ppermute | solution.py:53
  93.7 11.3 %collective-permute-start.5 = (bf16[256,512]{1,0:T(8,128)(2,1)S(1)}, bf16[256,512]{1,0:T(8,128)(2,1)S(1)}, u32[]{:S(2)}, u32[]{:S(2)}) collective-permute-start(bf16[256,512]{1,0:T(8,128)(2,1)S(1)} %collective-permute-done.4), channel_id=1, source_target_pairs={{0,4},{4,8},{8,12},{1,5},{5,9},{9,13},{2,6},{6,10},{10,14},{3,7},{... | collective-permute-start | bytes 786440 | tf_op jit(solution)/shard_map/ppermute | solution.py:53
  105.0 9.7 %collective-permute-done.5 = bf16[256,512]{1,0:T(8,128)(2,1)S(1)} collective-permute-done((bf16[256,512]{1,0:T(8,128)(2,1)S(1)}, bf16[256,512]{1,0:T(8,128)(2,1)S(1)}, u32[]{:S(2)}, u32[]{:S(2)}) %collective-permute-start.5) | collective-permute-done | bytes 262176 | tf_op jit(solution)/shard_map/ppermute | solution.py:53
  114.6 13.8 %collective-permute-start.6 = (bf16[256,512]{1,0:T(8,128)(2,1)S(1)}, bf16[256,512]{1,0:T(8,128)(2,1)S(1)}, u32[]{:S(2)}, u32[]{:S(2)}) collective-permute-start(bf16[256,512]{1,0:T(8,128)(2,1)S(1)} %collective-permute-done.5), channel_id=1, source_target_pairs={{0,4},{4,8},{8,12},{1,5},{5,9},{9,13},{2,6},{6,10},{10,14},{3,7},{... | collective-permute-start | bytes 786440 | tf_op jit(solution)/shard_map/ppermute | solution.py:53
  128.7 9.4 %collective-permute-done.6 = bf16[256,512]{1,0:T(8,128)(2,1)S(1)} collective-permute-done((bf16[256,512]{1,0:T(8,128)(2,1)S(1)}, bf16[256,512]{1,0:T(8,128)(2,1)S(1)}, u32[]{:S(2)}, u32[]{:S(2)}) %collective-permute-start.6) | collective-permute-done | bytes 262176 | tf_op jit(solution)/shard_map/ppermute | solution.py:53
  138.1 9.9 %collective-permute-start.7 = (bf16[256,512]{1,0:T(8,128)(2,1)S(1)}, bf16[256,512]{1,0:T(8,128)(2,1)S(1)}, u32[]{:S(2)}, u32[]{:S(2)}) collective-permute-start(bf16[256,512]{1,0:T(8,128)(2,1)S(1)} %collective-permute-done.6), channel_id=1, source_target_pairs={{0,4},{4,8},{8,12},{1,5},{5,9},{9,13},{2,6},{6,10},{10,14},{3,7},{... | collective-permute-start | bytes 786440 | tf_op jit(solution)/shard_map/ppermute | solution.py:53
  148.1 9.5 %collective-permute-done.7 = bf16[256,512]{1,0:T(8,128)(2,1)S(1)} collective-permute-done((bf16[256,512]{1,0:T(8,128)(2,1)S(1)}, bf16[256,512]{1,0:T(8,128)(2,1)S(1)}, u32[]{:S(2)}, u32[]{:S(2)}) %collective-permute-start.7) | collective-permute-done | bytes 262176 | tf_op jit(solution)/shard_map/ppermute | solution.py:53
  157.6 13.0 %collective-permute-start.8 = (bf16[256,512]{1,0:T(8,128)(2,1)S(1)}, bf16[256,512]{1,0:T(8,128)(2,1)S(1)}, u32[]{:S(2)}, u32[]{:S(2)}) collective-permute-start(bf16[256,512]{1,0:T(8,128)(2,1)S(1)} %collective-permute-done.7), channel_id=1, source_target_pairs={{0,4},{4,8},{8,12},{1,5},{5,9},{9,13},{2,6},{6,10},{10,14},{3,7},{... | collective-permute-start | bytes 786440 | tf_op jit(solution)/shard_map/ppermute | solution.py:53
  172.2 8.0 %collective-permute-done.8 = bf16[256,512]{1,0:T(8,128)(2,1)S(1)} collective-permute-done((bf16[256,512]{1,0:T(8,128)(2,1)S(1)}, bf16[256,512]{1,0:T(8,128)(2,1)S(1)}, u32[]{:S(2)}, u32[]{:S(2)}) %collective-permute-start.8) | collective-permute-done | bytes 262176 | tf_op jit(solution)/shard_map/ppermute | solution.py:53
  181.8 4.7 fusion.53
  186.5 6.0 %fusion.8 = bf16[256,4,256]{2,0,1:T(8,128)(2,1)S(1)} fusion(f32[4,256]{1,0:T(4,128)S(1)} %fusion.53, bf16[2304,512]{1,0:T(8,128)(2,1)} %copy-done.13, pred[256,2304]{0,1:T(8,128)(4,1)S(1)} %fusion.7, bf16[32,4,8,256]{3,2,1,0:T(8,128)(2,1)S(1)} %bitcast.79), kind=kOutput, calls=%fused_computation.17 | convolution fusion | flops 2427981056 | bytes 4001792 | tf_op jit(solution)/shard_map/htk,kd->thd/dot_general | solution.py:84
  192.5 6.9 %all-gather.3.cloned.1.call-done = bf16[1024,4096]{1,0:T(8,128)(2,1)} async-done(((bf16[1024,1024]{1,0:T(8,128)(2,1)}), bf16[1024,4096]{1,0:T(8,128)(2,1)}) %all-gather.3.cloned.1.call-update) | async-done | bytes 8388624 | tf_op jit(solution)/shard_map/all_gather | solution.py:129
  199.5 7.2 %convolution_convert_fusion = bf16[256,4096]{1,0:T(8,128)(2,1)} fusion(bf16[256,1024]{0,1:T(8,128)(2,1)S(1)} %bitcast.71, bf16[1024,4096]{1,0:T(8,128)(2,1)} %all-gather.3.cloned.1.call-done), kind=kOutput, calls=%fused_computation.6 | convolution fusion | flops 2148532224 | bytes 11010048 | tf_op jit(solution)/shard_map/dot_general | solution.py:127
  206.8 2.9 collective-permute-start.9
  209.7 32.0 %reduce-scatter.2.cloned.1.call-done = bf16[64,4096]{1,0:T(8,128)(2,1)} async-done(((bf16[256,4096]{1,0:T(8,128)(2,1)}), bf16[64,4096]{1,0:T(8,128)(2,1)}) %reduce-scatter.2.cloned.1.call-update) | async-done | bytes 524304 | tf_op jit(solution)/shard_map/reduce_scatter | solution.py:132
  244.8 3.4 collective-permute-start.10
  248.2 11.4 %collective-permute-done.9 = bf16[1024,1024]{1,0:T(8,128)(2,1)} collective-permute-done((bf16[1024,1024]{1,0:T(8,128)(2,1)S(1)}, bf16[1024,1024]{1,0:T(8,128)(2,1)}, u32[]{:S(2)}, u32[]{:S(2)}) %collective-permute-start.9) | collective-permute-done | bytes 2097184 | tf_op jit(solution)/shard_map/ppermute | solution.py:32
  259.7 4.4 broadcast_in_dim.103
  265.7 3.1 constant_dynamic-update-slice_fusion.11
  268.8 35.7 %collective-permute-done.10 = bf16[1024,1024]{1,0:T(8,128)(2,1)} collective-permute-done((bf16[1024,1024]{1,0:T(8,128)(2,1)S(1)}, bf16[1024,1024]{1,0:T(8,128)(2,1)}, u32[]{:S(2)}, u32[]{:S(2)}) %collective-permute-start.10) | collective-permute-done | bytes 2097184 | tf_op jit(solution)/shard_map/ppermute | solution.py:40
  304.5 3.1 constant_dynamic-update-slice_fusion.10
  307.6 39.7 %collective-permute-done.11 = bf16[1024,1024]{1,0:T(8,128)(2,1)} collective-permute-done((bf16[1024,1024]{1,0:T(8,128)(2,1)}, bf16[1024,1024]{1,0:T(8,128)(2,1)}, u32[]{:S(2)}, u32[]{:S(2)}) %collective-permute-start.11) | collective-permute-done | bytes 2097184 | tf_op jit(solution)/shard_map/ppermute | solution.py:32
  347.3 3.1 constant_dynamic-update-slice_fusion.9
  350.4 6.3 %convolution_convert_fusion.1 = bf16[256,1024]{1,0:T(8,128)(2,1)S(1)} fusion(bf16[256,4096]{1,0:T(8,128)(2,1)} %all-gather.5.cloned.1.call-done, bf16[4096,1024]{1,0:T(8,128)(2,1)} %constant_dynamic-update-slice_fusion.9), kind=kOutput, calls=%fused_computation.18 | convolution fusion | flops 2147745792 | bytes 11010048 | tf_op jit(solution)/shard_map/dot_general | solution.py:138
  356.8 1.9 collective-permute-start.12
  364.2 2.8 convert_multiply_fusion.2
  372.9 2.5 multiply_add_fusion.1
  375.4 1.7 slice.302
  380.3 1.9 multiply_add_fusion.2
  386.9 1.8 multiply_add_fusion.3
  434.4 1.7 slice.349
  449.4 2.7 pad.114
  452.3 2.3 fusion.24
  454.9 2.7 pad.130
  458.7 2.7 pad.129
  462.2 16.5 %while.10 = (s32[]{:T(128)}, f32[1024]{0:T(1024)S(1)}, f32[1024]{0:T(1024)S(1)}, f32[1024]{0:T(1024)S(1)}, s32[]{:T(128)}) while((s32[]{:T(128)}, f32[1024]{0:T(1024)S(1)}, f32[1024]{0:T(1024)S(1)}, f32[1024]{0:T(1024)S(1)}, s32[]{:T(128)}) %tuple.61), condition=%wide.region_6.7_spmd, body=%wide.region_5.6_spmd.sunk | while | flops 2050 | bytes 32869 | solution.py:183
  462.3 4.2 collective-permute-start
  467.8 4.2 collective-permute-start
  473.3 4.2 collective-permute-start
  478.8 2.8 add_convert_fusion
  (221 shorter events, 92.9 us)
Async XLA Ops:
  7.2 353.7 %copy-start = (bf16[4,256,256]{2,1,0:T(8,128)(2,1)S(1)}, bf16[4,256,256]{2,1,0:T(8,128)(2,1)}, u32[]{:S(2)}) copy-start(bf16[4,256,256]{2,1,0:T(8,128)(2,1)} %param.22) | copy-start | bytes 1572868
  7.2 121.3 %copy-start.14 = (s32[1024]{0:T(1024)S(1)}, s32[1024]{0:T(1024)}, u32[]{:S(2)}) copy-start(s32[1024]{0:T(1024)} %param.17) | copy-start | bytes 12292
  7.2 192.3 %all-gather.3.cloned.1.call-start = ((), (), s32[]{:S(2)}) async-start(), calls=%async_computation.1 | async-start | bytes 10485760 | tf_op jit(solution)/shard_map/all_gather | solution.py:129
  7.9 233.8 %reduce-scatter.2.cloned.1.call-start = ((), (), s32[]{:S(2)}) async-start(), calls=%async_computation.2 | async-start | bytes 2621440 | tf_op jit(solution)/shard_map/reduce_scatter | solution.py:132
  15.4 12.9 %collective-permute-start.1 = (bf16[256,512]{1,0:T(8,128)(2,1)S(1)}, bf16[256,512]{1,0:T(8,128)(2,1)S(1)}, u32[]{:S(2)}, u32[]{:S(2)}) collective-permute-start(bf16[256,512]{1,0:T(8,128)(2,1)S(1)} %all_gather.9), channel_id=1, source_target_pairs={{0,4},{4,8},{8,12},{1,5},{5,9},{9,13},{2,6},{6,10},{10,14},{3,7},{... | collective-permute-start | bytes 786440 | tf_op jit(solution)/shard_map/ppermute | solution.py:53
  28.3 19.7 %collective-permute-start.2 = (bf16[256,512]{1,0:T(8,128)(2,1)S(1)}, bf16[256,512]{1,0:T(8,128)(2,1)S(1)}, u32[]{:S(2)}, u32[]{:S(2)}) collective-permute-start(bf16[256,512]{1,0:T(8,128)(2,1)S(1)} %collective-permute-done.1), channel_id=1, source_target_pairs={{0,4},{4,8},{8,12},{1,5},{5,9},{9,13},{2,6},{6,10},{10,14},{3,7},{... | collective-permute-start | bytes 786440 | tf_op jit(solution)/shard_map/ppermute | solution.py:53
  48.0 23.8 %collective-permute-start.3 = (bf16[256,512]{1,0:T(8,128)(2,1)S(1)}, bf16[256,512]{1,0:T(8,128)(2,1)S(1)}, u32[]{:S(2)}, u32[]{:S(2)}) collective-permute-start(bf16[256,512]{1,0:T(8,128)(2,1)S(1)} %collective-permute-done.2), channel_id=1, source_target_pairs={{0,4},{4,8},{8,12},{1,5},{5,9},{9,13},{2,6},{6,10},{10,14},{3,7},{... | collective-permute-start | bytes 786440 | tf_op jit(solution)/shard_map/ppermute | solution.py:53
  71.8 21.9 %collective-permute-start.4 = (bf16[256,512]{1,0:T(8,128)(2,1)S(1)}, bf16[256,512]{1,0:T(8,128)(2,1)S(1)}, u32[]{:S(2)}, u32[]{:S(2)}) collective-permute-start(bf16[256,512]{1,0:T(8,128)(2,1)S(1)} %collective-permute-done.3), channel_id=1, source_target_pairs={{0,4},{4,8},{8,12},{1,5},{5,9},{9,13},{2,6},{6,10},{10,14},{3,7},{... | collective-permute-start | bytes 786440 | tf_op jit(solution)/shard_map/ppermute | solution.py:53
  93.7 21.0 %collective-permute-start.5 = (bf16[256,512]{1,0:T(8,128)(2,1)S(1)}, bf16[256,512]{1,0:T(8,128)(2,1)S(1)}, u32[]{:S(2)}, u32[]{:S(2)}) collective-permute-start(bf16[256,512]{1,0:T(8,128)(2,1)S(1)} %collective-permute-done.4), channel_id=1, source_target_pairs={{0,4},{4,8},{8,12},{1,5},{5,9},{9,13},{2,6},{6,10},{10,14},{3,7},{... | collective-permute-start | bytes 786440 | tf_op jit(solution)/shard_map/ppermute | solution.py:53
  114.6 23.4 %collective-permute-start.6 = (bf16[256,512]{1,0:T(8,128)(2,1)S(1)}, bf16[256,512]{1,0:T(8,128)(2,1)S(1)}, u32[]{:S(2)}, u32[]{:S(2)}) collective-permute-start(bf16[256,512]{1,0:T(8,128)(2,1)S(1)} %collective-permute-done.5), channel_id=1, source_target_pairs={{0,4},{4,8},{8,12},{1,5},{5,9},{9,13},{2,6},{6,10},{10,14},{3,7},{... | collective-permute-start | bytes 786440 | tf_op jit(solution)/shard_map/ppermute | solution.py:53
  138.1 19.5 %collective-permute-start.7 = (bf16[256,512]{1,0:T(8,128)(2,1)S(1)}, bf16[256,512]{1,0:T(8,128)(2,1)S(1)}, u32[]{:S(2)}, u32[]{:S(2)}) collective-permute-start(bf16[256,512]{1,0:T(8,128)(2,1)S(1)} %collective-permute-done.6), channel_id=1, source_target_pairs={{0,4},{4,8},{8,12},{1,5},{5,9},{9,13},{2,6},{6,10},{10,14},{3,7},{... | collective-permute-start | bytes 786440 | tf_op jit(solution)/shard_map/ppermute | solution.py:53
  157.6 22.6 %collective-permute-start.8 = (bf16[256,512]{1,0:T(8,128)(2,1)S(1)}, bf16[256,512]{1,0:T(8,128)(2,1)S(1)}, u32[]{:S(2)}, u32[]{:S(2)}) collective-permute-start(bf16[256,512]{1,0:T(8,128)(2,1)S(1)} %collective-permute-done.7), channel_id=1, source_target_pairs={{0,4},{4,8},{8,12},{1,5},{5,9},{9,13},{2,6},{6,10},{10,14},{3,7},{... | collective-permute-start | bytes 786440 | tf_op jit(solution)/shard_map/ppermute | solution.py:53
  180.4 1.4 copy-start.13
  181.8 4.7 copy-start.29
  199.5 7.3 %copy-start.2 = (bf16[1024,1024]{1,0:T(8,128)(2,1)S(1)}, bf16[1024,1024]{1,0:T(8,128)(2,1)}, u32[]{:S(2)}) copy-start(bf16[1024,1024]{1,0:T(8,128)(2,1)} %param.20) | copy-start | bytes 6291460
  206.7 35.0 %copy-start.5 = (bf16[64,4096]{1,0:T(8,128)(2,1)S(1)}, bf16[64,4096]{1,0:T(8,128)(2,1)}, u32[]{:S(2)}) copy-start(bf16[64,4096]{1,0:T(8,128)(2,1)} %param.18) | copy-start | bytes 1572868
  206.7 37.1 %copy-start.15 = (f32[4096]{0:T(1024)S(1)}, f32[4096]{0:T(1024)}, u32[]{:S(2)}) copy-start(f32[4096]{0:T(1024)} %param.27) | copy-start | bytes 49156
  206.7 52.9 %copy-start.26 = (s32[1024]{0:T(1024)S(1)}, s32[1024]{0:T(1024)}, u32[]{:S(2)}) copy-start(s32[1024]{0:T(1024)} %param.26) | copy-start | bytes 12292
  206.7 143.7 %all-gather.5.cloned.1.call-start = ((), (), s32[]{:S(2)}) async-start(), calls=%async_computation.3 | async-start | bytes 2621440 | tf_op jit(solution)/shard_map/all_gather | solution.py:136
  206.8 52.8 %collective-permute-start.9 = (bf16[1024,1024]{1,0:T(8,128)(2,1)S(1)}, bf16[1024,1024]{1,0:T(8,128)(2,1)}, u32[]{:S(2)}, u32[]{:S(2)}) collective-permute-start(bf16[1024,1024]{1,0:T(8,128)(2,1)S(1)} %copy-done.2), channel_id=1, source_target_pairs={{0,4},{4,8},{8,12},{12,0},{1,5},{5,9},{9,13},{13,1},{2,6},{6,10},{... | collective-permute-start | bytes 6291464 | tf_op jit(solution)/shard_map/ppermute | solution.py:32
  243.0 0.8 copy-start.3
  244.8 59.6 %collective-permute-start.10 = (bf16[1024,1024]{1,0:T(8,128)(2,1)S(1)}, bf16[1024,1024]{1,0:T(8,128)(2,1)}, u32[]{:S(2)}, u32[]{:S(2)}) collective-permute-start(bf16[1024,1024]{1,0:T(8,128)(2,1)S(1)} %copy-done.2), channel_id=1, source_target_pairs={{0,12},{4,0},{8,4},{12,8},{1,13},{5,1},{9,5},{13,9},{2,14},{6,2},{... | collective-permute-start | bytes 6291464 | tf_op jit(solution)/shard_map/ppermute | solution.py:40
  259.6 87.7 %collective-permute-start.11 = (bf16[1024,1024]{1,0:T(8,128)(2,1)}, bf16[1024,1024]{1,0:T(8,128)(2,1)}, u32[]{:S(2)}, u32[]{:S(2)}) collective-permute-start(bf16[1024,1024]{1,0:T(8,128)(2,1)} %collective-permute-done.9), channel_id=1, source_target_pairs={{0,4},{4,8},{8,12},{12,0},{1,5},{5,9},{9,13},{13,1},{2,6},{6,10},{... | collective-permute-start | bytes 6291464 | tf_op jit(solution)/shard_map/ppermute | solution.py:32
  264.1 1.5 copy-start.25
  356.8 3.3 collective-permute-start.12
  360.8 1.7 copy-start.6
  362.5 1.7 copy-start.27
  362.5 1.7 copy-start.28
  438.1 7.2 %copy-start.12 = (f32[3,1024]{1,0:T(4,128)S(1)}, f32[3,1024]{1,0:T(4,128)}, u32[]{:S(2)}) copy-start(f32[3,1024]{1,0:T(4,128)} %slice.341) | copy-start | bytes 36868
  438.1 7.3 %copy-start.24 = (f32[1,1024]{1,0:T(1,128)S(1)}, f32[1,1024]{1,0:T(1,128)}, u32[]{:S(2)}) copy-start(f32[1,1024]{1,0:T(1,128)} %slice.407) | copy-start | bytes 12292
  438.1 7.3 %copy-start.23 = (f32[1,1024]{1,0:T(1,128)S(1)}, f32[1,1024]{1,0:T(1,128)}, u32[]{:S(2)}) copy-start(f32[1,1024]{1,0:T(1,128)} %slice.381) | copy-start | bytes 12292
  438.1 7.4 %copy-start.10 = (f32[7,1024]{1,0:T(8,128)S(1)}, f32[7,1024]{1,0:T(8,128)}, u32[]{:S(2)}) copy-start(f32[7,1024]{1,0:T(8,128)} %slice.318) | copy-start | bytes 86020
  438.1 7.4 %copy-start.11 = (f32[7,1024]{1,0:T(8,128)S(1)}, f32[7,1024]{1,0:T(8,128)}, u32[]{:S(2)}) copy-start(f32[7,1024]{1,0:T(8,128)} %slice.343) | copy-start | bytes 86020
  438.1 9.0 %copy-start.8 = (f32[15,1024]{1,0:T(8,128)S(1)}, f32[15,1024]{1,0:T(8,128)}, u32[]{:S(2)}) copy-start(f32[15,1024]{1,0:T(8,128)} %slice.312) | copy-start | bytes 184324
  438.1 9.0 %copy-start.9 = (f32[15,1024]{1,0:T(8,128)S(1)}, f32[15,1024]{1,0:T(8,128)}, u32[]{:S(2)}) copy-start(f32[15,1024]{1,0:T(8,128)} %slice.345) | copy-start | bytes 184324
  441.2 6.8 %copy-start.7 = (f32[31,1024]{1,0:T(8,128)S(1)}, f32[31,1024]{1,0:T(8,128)}, u32[]{:S(2)}) copy-start(f32[31,1024]{1,0:T(8,128)} %slice.347) | copy-start | bytes 380932
  441.8 5.3 %copy-start.22 = (f32[1,1024]{1,0:T(1,128)S(1)}, f32[1,1024]{1,0:T(1,128)}, u32[]{:S(2)}) copy-start(f32[1,1024]{1,0:T(1,128)} %slice.405) | copy-start | bytes 12292
  445.5 2.6 copy-start.21
  447.1 1.2 copy-start.20
  448.0 1.0 copy-start.4
  448.2 0.9 copy-start.19
  449.1 3.0 copy-start.18
  452.3 2.3 copy-start.17
  454.6 3.0 copy-start.16
  454.8 6.6 %copy-start.1 = (f32[256,1024]{1,0:T(8,128)S(1)}, f32[256,1024]{1,0:T(8,128)}, u32[]{:S(2)}) copy-start(f32[256,1024]{1,0:T(8,128)} %pad.114) | copy-start | bytes 3145732
  462.3 5.5 %collective-permute-start = (f32[1024]{0:T(1024)S(1)}, f32[1024]{0:T(1024)S(1)}, u32[]{:S(2)}, u32[]{:S(2)}) collective-permute-start(f32[1024]{0:T(1024)S(1)} %multiply_add_fusion.9), channel_id=1, source_target_pairs={{0,4},{4,8},{8,12},{1,5},{5,9},{9,13},{2,6},{6,10},{10,14},{3,7},{... | collective-permute-start | bytes 12296 | tf_op jit(solution)/shard_map/while/body/eval_jaxpr/ppermute | solution.py:53
  467.8 5.5 %collective-permute-start = (f32[1024]{0:T(1024)S(1)}, f32[1024]{0:T(1024)S(1)}, u32[]{:S(2)}, u32[]{:S(2)}) collective-permute-start(f32[1024]{0:T(1024)S(1)} %multiply_add_fusion.9), channel_id=1, source_target_pairs={{0,4},{4,8},{8,12},{1,5},{5,9},{9,13},{2,6},{6,10},{10,14},{3,7},{... | collective-permute-start | bytes 12296 | tf_op jit(solution)/shard_map/while/body/eval_jaxpr/ppermute | solution.py:53
  473.3 5.5 %collective-permute-start = (f32[1024]{0:T(1024)S(1)}, f32[1024]{0:T(1024)S(1)}, u32[]{:S(2)}, u32[]{:S(2)}) collective-permute-start(f32[1024]{0:T(1024)S(1)} %multiply_add_fusion.9), channel_id=1, source_target_pairs={{0,4},{4,8},{8,12},{1,5},{5,9},{9,13},{2,6},{6,10},{10,14},{3,7},{... | collective-permute-start | bytes 12296 | tf_op jit(solution)/shard_map/while/body/eval_jaxpr/ppermute | solution.py:53
Sparse Core Ops, SparseCore 0:
  9.6 189.8 all-gather.2
  206.9 34.7 reduce-scatter.1
  245.0 22.5 all-gather.4
